TPU v7x, 512 devices: a whole 4x4x16 slice. The times are simulated.
512 devices in a mesh: gx: 16 (over y, z_hi, core), gy: 32 (over x, z_lo).
Axes of the slice: x: 4, y: 4, z: 16 (z_hi: 2, z_lo: 8; z = z_hi * 8 + z_lo), core: 2. Of those that a mesh axis runs over, the one named last changes fastest.
Arguments:
- tokens: bfloat16 [512, 16384], P('gy', 'gx'), may hold values from -6 to 6
- gate_weight: bfloat16 [16384, 26624], P('gx', 'gy'), may hold values from -0.046875 to 0.046875
- up_weight: bfloat16 [16384, 26624], P('gx', 'gy'), may hold values from -0.046875 to 0.046875
- down_weight: bfloat16 [26624, 16384], P('gy', 'gx'), may hold values from -0.0390625 to 0.0390625
Outputs:
- mixed: bfloat16 [512, 16384], P('gy', 'gx')
All inputs are finite; a program needn't handle non-finite values.
Results may differ from a plain program's by a relative error of at most 0.0049.
Values may be sent and summed in bfloat16 or wider, within the bound.
No kernel may reach another device: no remote copies, remote signals or barrier semaphores. Data moves between devices by JAX's collectives and lax.ppermute only.
A program may use at most 64 MiB of HBM per device.

v0:
```python
import jax
import jax.numpy as jnp
from jax import lax
from jax.sharding import PartitionSpec as P


def on_device(tokens, gate_weight, up_weight, down_weight):
    piece = lax.all_gather(tokens, "gy", axis=0, tiled=True)
    gate_part = jnp.dot(piece, gate_weight, preferred_element_type=jnp.float32)
    up_part = jnp.dot(piece, up_weight, preferred_element_type=jnp.float32)
    partial_value = jnp.stack([gate_part, up_part])
    summed = lax.psum(partial_value, "gx")
    hidden = (jax.nn.silu(summed[0]) * summed[1]).astype(jnp.bfloat16)
    mixed = lax.psum_scatter(
        jnp.dot(hidden, down_weight, preferred_element_type=jnp.float32),
        "gy",
        scatter_dimension=0,
        tiled=True,
    )
    return mixed.astype(jnp.bfloat16)


def solution(mesh):
    return jax.shard_map(
        on_device,
        mesh=mesh,
        in_specs=(P("gy", "gx"), P("gx", "gy"), P("gx", "gy"), P("gy", "gx")),
        out_specs=P("gy", "gx"),
        check_vma=False,
    )
```

profile of v0, /device:TPU:16, one launch (start us, length us, event | category | flops | bytes accessed | tf_op | source)
XLA Modules:
  0.0 865.9 jit_solution(11074020991371853969)
XLA Ops:
  6.5 0.0 copy-start
  6.5 0.0 all-gather.2.cloned.1.call-start
  6.5 0.7 all-gather.2.cloned.1.call-update
  7.3 0.0 copy-start.1
  7.3 0.0 all-reduce.2.cloned.1.call-start
  7.3 228.6 %all-gather.2.cloned.1.call-done = bf16[512,1024]{1,0:T(8,128)(2,1)} async-done(((bf16[16,1024]{1,0:T(8,128)(2,1)}), bf16[512,1024]{1,0:T(8,128)(2,1)}) %all-gather.2.cloned.1.call-update) | async-done | bytes 1048592 | tf_op jit(solution)/shard_map/all_gather | solution.py:8
  235.9 0.0 copy-start.2
  235.9 2.9 convolution_bitcast_fusion
  238.9 0.0 copy-done.1
  238.9 0.0 copy-done.2
  238.9 1.1 convolution_bitcast_fusion.1
  240.0 2.1 pad_maximum_fusion
  242.1 0.0 all-reduce.2.cloned.1.call-update
  242.1 0.0 reduce-scatter.2.cloned.1.call-start
  242.2 363.3 %all-reduce.2.cloned.1.call-done = f32[2,512,832]{1,2,0:T(8,128)} async-done(((f32[2,512,832]{1,2,0:T(8,128)}), f32[2,512,832]{1,2,0:T(8,128)}) %all-reduce.2.cloned.1.call-update) | async-done | bytes 3407888 | tf_op jit(solution)/shard_map/psum | solution.py:12
  605.5 0.0 copy-done
  605.5 4.7 fusion.2
  610.2 0.0 reduce-scatter.2.cloned.1.call-update
  610.2 247.7 %reduce-scatter.2.cloned.1.call-done = f32[16,1024]{1,0:T(8,128)} async-done(((f32[512,1024]{1,0:T(8,128)}), f32[16,1024]{1,0:T(8,128)}) %reduce-scatter.2.cloned.1.call-update) | async-done | bytes 65552 | tf_op jit(solution)/shard_map/reduce_scatter | solution.py:14
  857.9 1.5 convert_element_type.7
Async XLA Ops:
  6.5 599.0 %copy-start = (bf16[832,1024]{1,0:T(8,128)(2,1)S(1)}, bf16[832,1024]{1,0:T(8,128)(2,1)}, u32[]{:S(2)}) copy-start(bf16[832,1024]{1,0:T(8,128)(2,1)} %param.7) | copy-start | bytes 5111812
  6.5 229.4 %all-gather.2.cloned.1.call-start = ((), (), s32[]{:S(2)}) async-start(), calls=%async_computation.1 | async-start | bytes 1081344 | tf_op jit(solution)/shard_map/all_gather | solution.py:8
  7.3 231.6 %copy-start.1 = (bf16[1024,832]{0,1:T(8,128)(2,1)S(1)}, bf16[1024,832]{0,1:T(8,128)(2,1)}, u32[]{:S(2)}) copy-start(bf16[1024,832]{0,1:T(8,128)(2,1)} %param.5) | copy-start | bytes 5111812
  7.3 598.2 %all-reduce.2.cloned.1.call-start = ((), (), s32[]{:S(2)}) async-start(), calls=%async_computation.2 | async-start | bytes 6815744 | tf_op jit(solution)/shard_map/psum | solution.py:12
  235.9 3.0 copy-start.2
  242.1 615.7 %reduce-scatter.2.cloned.1.call-start = ((), (), s32[]{:S(2)}) async-start(), calls=%async_computation.3 | async-start | bytes 2162688 | tf_op jit(solution)/shard_map/reduce_scatter | solution.py:14
Sparse Core Ops, SparseCore 0:
  9.4 226.4 all-gather.1
  242.3 363.1 all-reduce.1
  610.3 247.5 reduce-scatter.1
where the time goes:
time: 866 us
  waiting for transfers between devices  840 us (97%)
  between operations  13.1 us (2%)
  matrix products  8.7 us (1%)
    psum x1, waiting for transfers between devices, on_device(): summed = lax.psum(partial_value, 'gx')  363 us
    reduce_scatter x1, waiting for transfers between devices, on_device(): lax.psum_scatter(jnp.dot(hidden, down_weight, preferred_element_type=jnp....  248 us
    all_gather x1, waiting for transfers between devices, on_device(): piece = lax.all_gather(tokens, 'gy', axis=0, tiled=True)  229 us
  transfers between devices with their start and end apart: 3, of which 3 were waited for; matrix products, arithmetic and copies ran while one was open for 0% of the time, Pallas kernels for 0%

commit v1 on v0

--- a/solution.py
+++ b/solution.py
@@ -5,7 +5,9 @@
 
 
 def on_device(tokens, gate_weight, up_weight, down_weight):
-    piece = lax.all_gather(tokens, "gy", axis=0, tiled=True)
+    piece = jnp.concatenate(
+        lax.all_to_all(jnp.stack([tokens] * lax.axis_size("gy")), "gy", 0, 0), axis=0
+    )
     gate_part = jnp.dot(piece, gate_weight, preferred_element_type=jnp.float32)
     up_part = jnp.dot(piece, up_weight, preferred_element_type=jnp.float32)
     partial_value = jnp.stack([gate_part, up_part])

time: 866 us -> 702 us (0.81)
  the two profiles are of different devices: /device:TPU:16 before, /device:TPU:8 now
where the time goes in v1:
time: 702 us
  waiting for transfers between devices  610 us (87%)
  blocking collectives  66.4 us (9%)
  between operations  13.4 us (2%)
    psum x1, waiting for transfers between devices, on_device(): summed = lax.psum(partial_value, 'gx')  369 us
    reduce_scatter x1, waiting for transfers between devices, on_device(): lax.psum_scatter(jnp.dot(hidden, down_weight, preferred_element_type=jnp....  242 us
    all_to_all x1, blocking collectives, on_device(): lax.all_to_all(jnp.stack([tokens] * lax.axis_size('gy')), 'gy', 0, 0)  66.4 us
  transfers between devices with their start and end apart: 2, of which 2 were waited for; matrix products, arithmetic and copies ran while one was open for 0% of the time, Pallas kernels for 0%

profile of v1, /device:TPU:8, one launch (start us, length us, event | category | flops | bytes accessed | tf_op | source)
XLA Modules:
  0.0 702.0 jit_solution(4646711859678384553)
XLA Ops:
  6.5 0.0 copy-start
  6.5 0.0 copy-start.1
  6.5 0.0 all-reduce.2.cloned.1.call-start
  6.5 1.0 stack.8
  7.6 66.4 %all_to_all.5 = bf16[32,16,1024]{2,1,0:T(8,128)(2,1)S(1)} all-to-all(bf16[32,16,1024]{2,1,0:T(8,128)(2,1)S(1)} %stack.8), channel_id=1, replica_groups=mesh['gx'=16,'gy'=32] {'gy'}, dimensions={0} | all-to-all | bytes 2097152 | tf_op jit(solution)/shard_map/all_to_all | solution.py:9
  73.9 0.0 copy-done.1
  73.9 0.0 copy-start.2
  73.9 1.1 convolution_bitcast_fusion
  75.0 0.4 copy-done.2
  75.4 1.1 convolution_bitcast_fusion.1
  76.5 2.1 pad_maximum_fusion
  78.6 0.0 all-reduce.2.cloned.1.call-update
  78.6 0.0 reduce-scatter.2.cloned.1.call-start
  78.7 368.7 %all-reduce.2.cloned.1.call-done = f32[2,512,832]{1,2,0:T(8,128)} async-done(((f32[2,512,832]{1,2,0:T(8,128)}), f32[2,512,832]{1,2,0:T(8,128)}) %all-reduce.2.cloned.1.call-update) | async-done | bytes 3407888 | tf_op jit(solution)/shard_map/psum | solution.py:14
  447.3 0.0 copy-done
  447.3 4.7 fusion.2
  452.0 0.0 reduce-scatter.2.cloned.1.call-update
  452.0 241.6 %reduce-scatter.2.cloned.1.call-done = f32[16,1024]{1,0:T(8,128)} async-done(((f32[512,1024]{1,0:T(8,128)}), f32[16,1024]{1,0:T(8,128)}) %reduce-scatter.2.cloned.1.call-update) | async-done | bytes 65552 | tf_op jit(solution)/shard_map/reduce_scatter | solution.py:16
  693.7 1.5 convert_element_type.7
Async XLA Ops:
  6.5 440.8 %copy-start = (bf16[832,1024]{1,0:T(8,128)(2,1)S(1)}, bf16[832,1024]{1,0:T(8,128)(2,1)}, u32[]{:S(2)}) copy-start(bf16[832,1024]{1,0:T(8,128)(2,1)} %param.7) | copy-start | bytes 5111812
  6.5 67.4 %copy-start.1 = (bf16[1024,832]{0,1:T(8,128)(2,1)S(1)}, bf16[1024,832]{0,1:T(8,128)(2,1)}, u32[]{:S(2)}) copy-start(bf16[1024,832]{0,1:T(8,128)(2,1)} %param.6) | copy-start | bytes 5111812
  6.5 440.8 %all-reduce.2.cloned.1.call-start = ((), (), s32[]{:S(2)}) async-start(), calls=%async_computation.2 | async-start | bytes 6815744 | tf_op jit(solution)/shard_map/psum | solution.py:14
  73.9 1.5 copy-start.2
  78.6 615.0 %reduce-scatter.2.cloned.1.call-start = ((), (), s32[]{:S(2)}) async-start(), calls=%async_computation.3 | async-start | bytes 2162688 | tf_op jit(solution)/shard_map/reduce_scatter | solution.py:16
Sparse Core Ops, SparseCore 0:
  78.7 368.5 all-reduce.1
  452.2 241.4 reduce-scatter.1
